TPU v7x, 32 devices: a whole 2x2x4 slice. The times are simulated.
32 devices in a mesh: dp: 16 (over z, y, core), tensor: 2 (over x).
Axes of the slice: x: 2, y: 2, z: 4, core: 2. Of those that a mesh axis runs over, the one named last changes fastest.
Arguments:
- layer_input: float32 [8192, 1024], P(('dp', 'tensor')), may hold values from -6 to 6
- segment_ids: int32 [16, 512], P('dp'), may hold values from 0 to 3, never falling along the last dimension, each value on 1 to 256 neighbouring positions
- norm1_gain: bfloat16 [1024], P('dp'), may hold values from 0.25 to 1.75
- norm1_shift: bfloat16 [1024], P('dp'), may hold values from -3 to 3
- qkv_weight: bfloat16 [1024, 3072], P('dp', 'tensor'), may hold values from -1 to 1
- qkv_bias: bfloat16 [2048], P(('tensor', 'dp')), may hold values from -3 to 3
- dense_weight: bfloat16 [1024, 1024], P('dp', 'tensor'), may hold values from -0.75 to 0.75
- dense_bias: bfloat16 [1024], P('dp'), may hold values from -3 to 3
- norm2_gain: bfloat16 [1024], P('dp'), may hold values from 0.25 to 1.75
- norm2_shift: bfloat16 [1024], P('dp'), may hold values from -3 to 3
- inner_weight: bfloat16 [1024, 4096], P('dp', 'tensor'), may hold values from -0.1875 to 0.1875
- inner_bias: bfloat16 [4096], P(('tensor', 'dp')), may hold values from -3 to 3
- outer_weight: bfloat16 [1024, 4096], P('dp', 'tensor'), may hold values from -0.1875 to 0.1875
- outer_bias: bfloat16 [1024], P('dp'), may hold values from -3 to 3
- out_cotangent: float32 [8192, 1024], P(('dp', 'tensor')), may hold values from -6 to 6
Outputs:
- layer_output: float32 [8192, 1024], P(('dp', 'tensor'))
- input_grad: float32 [8192, 1024], P(('dp', 'tensor'))
- norm1_gain_grad: float32 [1024], P('dp')
- norm1_shift_grad: float32 [1024], P('dp')
- qkv_weight_grad: float32 [1024, 3072], P('dp', 'tensor')
- qkv_bias_grad: float32 [2048], P(('tensor', 'dp'))
- dense_weight_grad: float32 [1024, 1024], P('dp', 'tensor')
- dense_bias_grad: float32 [1024], P('dp')
- norm2_gain_grad: float32 [1024], P('dp')
- norm2_shift_grad: float32 [1024], P('dp')
- inner_weight_grad: float32 [1024, 4096], P('dp', 'tensor')
- inner_bias_grad: float32 [4096], P(('tensor', 'dp'))
- outer_weight_grad: float32 [1024, 4096], P('dp', 'tensor')
- outer_bias_grad: float32 [1024], P('dp')
Inputs may be any that keep to these rules, and one draw needn't show every extreme that they name: `segment_ids`: along each row the ids never fall; each segment spans 1 to 256 positions, and one spans exactly 256.
All inputs are finite; a program needn't handle non-finite values.
Results may differ from a plain program's by a relative error of at most 0.024.
Values may be sent and summed in bfloat16 or wider, within the bound.
No kernel may reach another device: no remote copies, remote signals or barrier semaphores. Data moves between devices by JAX's collectives and lax.ppermute only.
A program may use at most 128 MiB of HBM per device.

v0:
```python
import jax
import jax.numpy as jnp
from jax import lax
from jax.sharding import PartitionSpec as P

H = 16
HD = 64
EPSILON = 1e-05
GELU_C = 0.7978845608028654
GELU_K = 0.044715


def layer_norm(row_data, gain, shift):
    row_mean = jnp.mean(row_data, axis=-1, keepdims=True)
    centered = row_data - row_mean
    row_var = jnp.mean(centered * centered, axis=-1, keepdims=True)
    inv_std = lax.rsqrt(row_var + EPSILON)
    normed = centered * inv_std
    return (normed * gain.astype(jnp.float32) + shift.astype(jnp.float32), normed, inv_std)


def norm_back(grad_out, normed, inv_std, gain):
    scaled = grad_out * gain.astype(jnp.float32)
    mean_grad = jnp.mean(scaled, axis=-1, keepdims=True)
    mean_cross = jnp.mean(scaled * normed, axis=-1, keepdims=True)
    return inv_std * (scaled - mean_grad - normed * mean_cross)


def gelu_parts(pre_act):
    cubed_term = pre_act * pre_act * pre_act
    tangent = jnp.tanh(GELU_C * (pre_act + GELU_K * cubed_term))
    result = 0.5 * pre_act * (1.0 + tangent)
    derivative = 0.5 * (1.0 + tangent) + 0.5 * pre_act * (1.0 - tangent * tangent) * GELU_C * (
        1.0 + 3.0 * GELU_K * pre_act * pre_act
    )
    return (result, derivative)


def rows_product(left, right):
    return lax.dot_general(
        left, right, (((0,), (0,)), ((), ())), preferred_element_type=jnp.float32
    )


def cross_product(left, right):
    return lax.dot_general(
        left, right, (((1,), (1,)), ((), ())), preferred_element_type=jnp.float32
    )


def block_scores(query_block, key_rows, segment_row, head_slopes):
    block_len = query_block.shape[0]
    scores = jnp.einsum(
        "bhe,the->hbt", query_block, key_rows, preferred_element_type=jnp.float32
    ) * HD ** (-0.5)
    row_pos = jnp.arange(block_len, dtype=jnp.int32)
    col_pos = jnp.arange(key_rows.shape[0], dtype=jnp.int32)
    allowed = (col_pos[None, :] <= row_pos[:, None]) & (
        segment_row[:, None] == segment_row[None, :]
    )
    distance = (row_pos[:, None] - col_pos[None, :]).astype(jnp.float32)
    scores = scores - head_slopes[:, None, None] * distance[None]
    return jnp.where(allowed[None], scores, -1e30)


def attend_forward(query_rows, key_rows, value_rows, segment_row, head_slopes):
    scores = block_scores(query_rows, key_rows, segment_row, head_slopes)
    row_max = jnp.max(scores, axis=-1, keepdims=True)
    log_total = row_max + jnp.log(jnp.sum(jnp.exp(scores - row_max), axis=-1, keepdims=True))
    attn_probs = jnp.exp(scores - log_total).astype(jnp.bfloat16)
    context = jnp.einsum("hbt,the->bhe", attn_probs, value_rows, preferred_element_type=jnp.float32)
    outputs = context.astype(jnp.bfloat16)
    return (outputs, log_total)


def attend_backward(
    query_rows, key_rows, value_rows, context, context_grad, log_total, segment_row, head_slopes
):
    scale = HD ** (-0.5)
    scores = block_scores(query_rows, key_rows, segment_row, head_slopes)
    probs = jnp.exp(scores - log_total)
    probs_low = probs.astype(jnp.bfloat16)
    value_grad = jnp.einsum(
        "hbt,bhe->the", probs_low, context_grad, preferred_element_type=jnp.float32
    )
    prob_grad = jnp.einsum(
        "bhe,the->hbt", context_grad, value_rows, preferred_element_type=jnp.float32
    )
    delta = jnp.sum(context_grad.astype(jnp.float32) * context.astype(jnp.float32), axis=-1)
    score_grad = (probs * (prob_grad - jnp.transpose(delta)[:, :, None])).astype(jnp.bfloat16)
    query_parts = (
        jnp.einsum("hbt,the->bhe", score_grad, key_rows, preferred_element_type=jnp.float32) * scale
    )
    key_grad = (
        jnp.einsum("hbt,bhe->the", score_grad, query_rows, preferred_element_type=jnp.float32)
        * scale
    )
    return (query_parts, key_grad, value_grad)


def on_device(
    layer_input,
    segment_ids,
    norm1_gain,
    norm1_shift,
    qkv_weight,
    qkv_bias,
    dense_weight,
    dense_bias,
    norm2_gain,
    norm2_shift,
    inner_weight,
    inner_bias,
    outer_weight,
    outer_bias,
    out_cotangent,
):
    gathered = (
        lax.all_gather(norm1_gain, "dp", axis=0, tiled=True),
        lax.all_gather(norm1_shift, "dp", axis=0, tiled=True),
        lax.all_gather(qkv_weight, "dp", axis=0, tiled=True),
        lax.all_gather(qkv_bias, "dp", axis=0, tiled=True),
        lax.all_gather(dense_weight, "dp", axis=0, tiled=True),
        lax.all_gather(dense_bias, "dp", axis=0, tiled=True),
        lax.all_gather(norm2_gain, "dp", axis=0, tiled=True),
        lax.all_gather(norm2_shift, "dp", axis=0, tiled=True),
        lax.all_gather(inner_weight, "dp", axis=0, tiled=True),
        lax.all_gather(inner_bias, "dp", axis=0, tiled=True),
        lax.all_gather(outer_weight, "dp", axis=0, tiled=True),
        lax.all_gather(outer_bias, "dp", axis=0, tiled=True),
    )
    (
        gain_one,
        shift_one,
        qkv_full,
        qkv_bias_full,
        dense_full,
        dense_bias_full,
        gain_two,
        shift_two,
        inner_full,
        inner_bias_full,
        outer_full,
        outer_bias_full,
    ) = gathered
    local_heads = qkv_full.shape[1] // (3 * HD)
    head_index = lax.axis_index("tensor") * local_heads + jnp.arange(local_heads, dtype=jnp.int32)
    head_slopes = jnp.exp2(-8.0 * (head_index.astype(jnp.float32) + 1.0) / H)
    segment_row = segment_ids[0]
    bias_pairs = qkv_bias_full.astype(jnp.float32).reshape(local_heads, 2, HD)
    bias_three = jnp.stack(
        [bias_pairs[:, 0], jnp.zeros_like(bias_pairs[:, 0]), bias_pairs[:, 1]], axis=1
    ).reshape(-1)
    normed_one, hat_one, inv_one = layer_norm(layer_input, gain_one, shift_one)
    norm_rows = lax.all_gather(normed_one.astype(jnp.bfloat16), "tensor", axis=0, tiled=True)
    group_rows = norm_rows.shape[0]
    projected = (
        jnp.dot(norm_rows, qkv_full, preferred_element_type=jnp.float32) + bias_three
    ).astype(jnp.bfloat16)
    projected = projected.reshape(group_rows, local_heads, 3, HD)
    query_rows = projected[:, :, 0]
    key_rows = projected[:, :, 1]
    value_rows = projected[:, :, 2]
    context, log_total = attend_forward(query_rows, key_rows, value_rows, segment_row, head_slopes)
    context_flat = context.reshape(group_rows, local_heads * HD)
    attn_part = lax.psum_scatter(
        cross_product(context_flat, dense_full).astype(jnp.bfloat16),
        "tensor",
        scatter_dimension=0,
        tiled=True,
    ).astype(jnp.float32)
    middle = layer_input + attn_part + dense_bias_full.astype(jnp.float32)
    normed_two, hat_two, inv_two = layer_norm(middle, gain_two, shift_two)
    mid_rows = lax.all_gather(normed_two.astype(jnp.bfloat16), "tensor", axis=0, tiled=True)
    pre_act = jnp.dot(
        mid_rows, inner_full, preferred_element_type=jnp.float32
    ) + inner_bias_full.astype(jnp.float32)
    act_value, act_slope = gelu_parts(pre_act)
    act_low = act_value.astype(jnp.bfloat16)
    layer_output = (
        middle
        + lax.psum_scatter(
            cross_product(act_low, outer_full).astype(jnp.bfloat16),
            "tensor",
            scatter_dimension=0,
            tiled=True,
        ).astype(jnp.float32)
        + outer_bias_full.astype(jnp.float32)
    )
    back_set = (
        lax.all_gather(norm1_gain, "dp", axis=0, tiled=True),
        lax.all_gather(qkv_weight, "dp", axis=0, tiled=True),
        lax.all_gather(dense_weight, "dp", axis=0, tiled=True),
        lax.all_gather(norm2_gain, "dp", axis=0, tiled=True),
        lax.all_gather(inner_weight, "dp", axis=0, tiled=True),
        lax.all_gather(outer_weight, "dp", axis=0, tiled=True),
    )
    gain_back_one, qkv_back, dense_back, gain_back_two, inner_back, outer_back = back_set
    cot_rows = lax.all_gather(out_cotangent.astype(jnp.bfloat16), "tensor", axis=0, tiled=True)
    outer_grad = rows_product(cot_rows, act_low)
    pre_grad = jnp.dot(cot_rows, outer_back, preferred_element_type=jnp.float32) * act_slope
    inner_bias_grad = jnp.sum(pre_grad, axis=0)
    pre_low = pre_grad.astype(jnp.bfloat16)
    inner_grad = rows_product(mid_rows, pre_low)
    mid_grad = lax.psum_scatter(
        cross_product(pre_low, inner_back).astype(jnp.bfloat16),
        "tensor",
        scatter_dimension=0,
        tiled=True,
    ).astype(jnp.float32)
    gain_two_grad = jnp.sum(mid_grad * hat_two, axis=0)
    shift_two_grad = jnp.sum(mid_grad, axis=0)
    middle_grad = out_cotangent + norm_back(mid_grad, hat_two, inv_two, gain_back_two)
    dense_bias_grad = jnp.sum(middle_grad, axis=0)
    outer_bias_grad = jnp.sum(out_cotangent, axis=0)
    middle_rows = lax.all_gather(middle_grad.astype(jnp.bfloat16), "tensor", axis=0, tiled=True)
    dense_grad = rows_product(middle_rows, context_flat)
    context_grad = jnp.dot(middle_rows, dense_back, preferred_element_type=jnp.float32).astype(
        jnp.bfloat16
    )
    context_grad = context_grad.reshape(group_rows, local_heads, HD)
    query_grad, key_grad, value_grad = attend_backward(
        query_rows, key_rows, value_rows, context, context_grad, log_total, segment_row, head_slopes
    )
    qkv_grad = jnp.stack([query_grad, key_grad, value_grad], axis=2).reshape(
        group_rows, local_heads * 3 * HD
    )
    bias_sums = jnp.sum(qkv_grad, axis=0).reshape(local_heads, 3, HD)
    qkv_bias_grad = jnp.stack([bias_sums[:, 0], bias_sums[:, 2]], axis=1).reshape(-1)
    qkv_low = qkv_grad.astype(jnp.bfloat16)
    qkv_weight_grad = rows_product(norm_rows, qkv_low)
    first_grad = lax.psum_scatter(
        cross_product(qkv_low, qkv_back).astype(jnp.bfloat16),
        "tensor",
        scatter_dimension=0,
        tiled=True,
    ).astype(jnp.float32)
    gain_one_grad = jnp.sum(first_grad * hat_one, axis=0)
    shift_one_grad = jnp.sum(first_grad, axis=0)
    input_grad = middle_grad + norm_back(first_grad, hat_one, inv_one, gain_back_one)
    small_sums = lax.psum(
        (
            gain_one_grad,
            shift_one_grad,
            dense_bias_grad,
            gain_two_grad,
            shift_two_grad,
            outer_bias_grad,
        ),
        "tensor",
    )
    everything = (
        lax.psum_scatter(
            small_sums[0].astype(jnp.bfloat16), "dp", scatter_dimension=0, tiled=True
        ).astype(jnp.float32),
        lax.psum_scatter(
            small_sums[1].astype(jnp.bfloat16), "dp", scatter_dimension=0, tiled=True
        ).astype(jnp.float32),
        lax.psum_scatter(
            qkv_weight_grad.astype(jnp.bfloat16), "dp", scatter_dimension=0, tiled=True
        ).astype(jnp.float32),
        lax.psum_scatter(
            qkv_bias_grad.astype(jnp.bfloat16), "dp", scatter_dimension=0, tiled=True
        ).astype(jnp.float32),
        lax.psum_scatter(
            dense_grad.astype(jnp.bfloat16), "dp", scatter_dimension=0, tiled=True
        ).astype(jnp.float32),
        lax.psum_scatter(
            small_sums[2].astype(jnp.bfloat16), "dp", scatter_dimension=0, tiled=True
        ).astype(jnp.float32),
        lax.psum_scatter(
            small_sums[3].astype(jnp.bfloat16), "dp", scatter_dimension=0, tiled=True
        ).astype(jnp.float32),
        lax.psum_scatter(
            small_sums[4].astype(jnp.bfloat16), "dp", scatter_dimension=0, tiled=True
        ).astype(jnp.float32),
        lax.psum_scatter(
            inner_grad.astype(jnp.bfloat16), "dp", scatter_dimension=0, tiled=True
        ).astype(jnp.float32),
        lax.psum_scatter(
            inner_bias_grad.astype(jnp.bfloat16), "dp", scatter_dimension=0, tiled=True
        ).astype(jnp.float32),
        lax.psum_scatter(
            outer_grad.astype(jnp.bfloat16), "dp", scatter_dimension=0, tiled=True
        ).astype(jnp.float32),
        lax.psum_scatter(
            small_sums[5].astype(jnp.bfloat16), "dp", scatter_dimension=0, tiled=True
        ).astype(jnp.float32),
    )
    return (
        layer_output,
        input_grad,
        everything[0],
        everything[1],
        everything[2],
        everything[3],
        everything[4],
        everything[5],
        everything[6],
        everything[7],
        everything[8],
        everything[9],
        everything[10],
        everything[11],
    )


def solution(mesh):
    in_specs = (
        P(("dp", "tensor"), None),
        P("dp", None),
        P("dp"),
        P("dp"),
        P("dp", "tensor"),
        P(("tensor", "dp")),
        P("dp", "tensor"),
        P("dp"),
        P("dp"),
        P("dp"),
        P("dp", "tensor"),
        P(("tensor", "dp")),
        P("dp", "tensor"),
        P("dp"),
        P(("dp", "tensor"), None),
    )
    out_specs = (
        P(("dp", "tensor"), None),
        P(("dp", "tensor"), None),
        P("dp"),
        P("dp"),
        P("dp", "tensor"),
        P(("tensor", "dp")),
        P("dp", "tensor"),
        P("dp"),
        P("dp"),
        P("dp"),
        P("dp", "tensor"),
        P(("tensor", "dp")),
        P("dp", "tensor"),
        P("dp"),
    )
    return jax.shard_map(
        on_device, mesh=mesh, in_specs=in_specs, out_specs=out_specs, check_vma=False
    )
```

profile of v0, /device:TPU:0, one launch (start us, length us, event | category | flops | bytes accessed | tf_op | source)
XLA Modules:
  0.0 754.2 jit_solution(11036563063567816782)
XLA Ops:
  14.3 63.0 %all-reduce.17 = (bf16[1024]{0:T(1024)(128)(2,1)S(1)}, bf16[1024]{0:T(1024)(128)(2,1)S(1)}, bf16[1024]{0:T(1024)(128)(2,1)S(1)}, bf16[1024]{0:T(1024)(128)(2,1)S...) all-reduce(bf16[1024]{0:T(1024)(128)(2,1)S(1)} %dynamic-update-slic, ...), channel_id=1, replica_groups=mesh['dp'=16,'tensor'=2] {'dp'}, use_global_device_ids=true, to_apply=%add.1 | all-reduce | flops 6144 | bytes 24576
  84.6 16.5 %all-gather.10.cloned.1.call-done = bf16[512,1024]{1,0:T(8,128)(2,1)} async-done(((bf16[256,1024]{1,0:T(8,128)(2,1)}), bf16[512,1024]{1,0:T(8,128)(2,1)}) %all-gather.10.cloned.1.call-update) | async-done | bytes 1048592 | tf_op jit(solution)/shard_map/all_gather | solution.py:155
  101.1 47.8 %all-gather.12.cloned.1.call-done = bf16[1024,1536]{1,0:T(8,128)(2,1)} async-done(((bf16[64,1536]{1,0:T(8,128)(2,1)}), bf16[1024,1536]{1,0:T(8,128)(2,1)}) %all-gather.12.cloned.1.call-update) | async-done | bytes 3145744 | tf_op jit(solution)/shard_map/all_gather | solution.py:121
  162.9 24.4 %all-gather.14.cloned.1.call-done = bf16[1024,512]{1,0:T(8,128)(2,1)} async-done(((bf16[64,512]{1,0:T(8,128)(2,1)}), bf16[1024,512]{1,0:T(8,128)(2,1)}) %all-gather.14.cloned.1.call-update) | async-done | bytes 1048592 | tf_op jit(solution)/shard_map/all_gather | solution.py:123
  191.0 18.8 %reduce-scatter.11.cloned.1.call-done = bf16[256,1024]{1,0:T(8,128)(2,1)} async-done(((bf16[512,1024]{1,0:T(8,128)(2,1)}), bf16[256,1024]{1,0:T(8,128)(2,1)}) %reduce-scatter.11.cloned.1.call-update) | async-done | bytes 524304 | tf_op jit(solution)/shard_map/reduce_scatter | solution.py:166
  214.2 22.0 %all-gather = bf16[16,1,128]{2,1,0:T(2,128)(2,1)S(1)} all-gather(bf16[1,1,128]{2,1,0:T(2,128)(2,1)S(1)} %bitcast.96), channel_id=1, replica_groups=mesh['dp'=16,'tensor'=2] {'dp'}, dimensions={0}, use_global_device_ids=true | all-gather | bytes 4352 | tf_op jit(solution)/shard_map/all_gather | solution.py:128
  236.2 26.1 %all-gather.18.cloned.1.call-done = bf16[1024,2048]{1,0:T(8,128)(2,1)} async-done(((bf16[64,2048]{1,0:T(8,128)(2,1)}), bf16[1024,2048]{1,0:T(8,128)(2,1)}) %all-gather.18.cloned.1.call-update) | async-done | bytes 4194320 | tf_op jit(solution)/shard_map/all_gather | solution.py:127
  262.3 21.8 %all-gather.16.cloned.1.call-done = bf16[512,1024]{1,0:T(8,128)(2,1)} async-done(((bf16[256,1024]{1,0:T(8,128)(2,1)}), bf16[512,1024]{1,0:T(8,128)(2,1)}) %all-gather.16.cloned.1.call-update) | async-done | bytes 1048592 | tf_op jit(solution)/shard_map/all_gather | solution.py:174
  284.1 6.8 fusion.44
  290.9 16.6 %all-gather.22.cloned.1.call-done = bf16[512,1024]{1,0:T(8,128)(2,1)} async-done(((bf16[256,1024]{1,0:T(8,128)(2,1)}), bf16[512,1024]{1,0:T(8,128)(2,1)}) %all-gather.22.cloned.1.call-update) | async-done | bytes 1048592 | tf_op jit(solution)/shard_map/all_gather | solution.py:199
  307.5 52.6 %all-gather.20.cloned.1.call-done = bf16[1024,2048]{1,0:T(8,128)(2,1)} async-done(((bf16[64,2048]{1,0:T(8,128)(2,1)}), bf16[1024,2048]{1,0:T(8,128)(2,1)}) %all-gather.20.cloned.1.call-update) | async-done | bytes 4194320 | tf_op jit(solution)/shard_map/all_gather | solution.py:129
  360.1 8.4 %fusion.43 = (bf16[2048]{0:T(1024)(128)(2,1)S(1)}, bf16[512,2048]{1,0:T(8,128)(2,1)S(1)}) fusion(f32[512,2048]{1,0:T(8,128)} %fusion.44, f32[2048]{0:T(1024)S(1)} %bitcast.93, bf16[512,1024]{1,0:T(8,128)(2,1)} %all-gather.22.cloned.1.call-done, bf16[1024,2048]{1,0:T(8,128)(2,1)} %all-gather.20.cloned.1.call-done), kind=kOutput, calls=%fused_computation.102 | convolution fusion | flops 2169501696 | bytes 11546624 | tf_op jit(solution)/shard_map/dot_general | solution.py:201
  373.3 19.0 %reduce-scatter.15.cloned.1.call-done = bf16[256,1024]{1,0:T(8,128)(2,1)} async-done(((bf16[512,1024]{1,0:T(8,128)(2,1)}), bf16[256,1024]{1,0:T(8,128)(2,1)}) %reduce-scatter.15.cloned.1.call-update) | async-done | bytes 524304 | tf_op jit(solution)/shard_map/reduce_scatter | solution.py:205
  396.6 21.4 %all-gather.24.cloned.1.call-done = bf16[512,1024]{1,0:T(8,128)(2,1)} async-done(((bf16[256,1024]{1,0:T(8,128)(2,1)}), bf16[512,1024]{1,0:T(8,128)(2,1)}) %all-gather.24.cloned.1.call-update) | async-done | bytes 1048592 | tf_op jit(solution)/shard_map/all_gather | solution.py:216
  438.9 7.3 convolution_convert_fusion.6
  446.4 7.9 %convert_bitcast_fusion = bf16[1024,2048]{0,1:T(8,128)(2,1)} fusion(bf16[512,1024]{1,0:T(8,128)(2,1)} %all-gather.22.cloned.1.call-done, f32[512,2048]{1,0:T(8,128)} %fusion.44, f32[2048]{0:T(1024)S(1)} %bitcast.95), kind=kOutput, calls=%fused_computation.15 | convolution fusion | flops 2160066560 | bytes 9445376 | tf_op jit(solution)/shard_map/dot_general | solution.py:40
  454.3 6.5 copy.77
  460.9 6.3 convolution_convert_fusion
  480.9 20.5 %reduce-scatter.17.cloned.1.call-done = bf16[256,1024]{1,0:T(8,128)(2,1)} async-done(((bf16[512,1024]{1,0:T(8,128)(2,1)}), bf16[256,1024]{1,0:T(8,128)(2,1)}) %reduce-scatter.17.cloned.1.call-update) | async-done | bytes 524304 | tf_op jit(solution)/shard_map/reduce_scatter | solution.py:232
  503.0 7.1 all-reduce.15
  510.1 60.0 %all-reduce.16 = (bf16[1024]{0:T(1024)(128)(2,1)S(1)}, bf16[1024]{0:T(1024)(128)(2,1)S(1)}, bf16[1024]{0:T(1024)(128)(2,1)S(1)}, bf16[1024]{0:T(1024)(128)(2,1)S...) all-reduce(bf16[1024]{0:T(1024)(128)(2,1)S(1)} %dynamic-update-slic, ...), channel_id=1, replica_groups=mesh['dp'=16,'tensor'=2] {'dp'}, use_global_device_ids=true, to_apply=%add.6 | all-reduce | flops 10240 | bytes 40960
  579.4 21.6 %reduce-scatter.25.cloned.1.call-done = bf16[64,2048]{1,0:T(8,128)(2,1)} async-done(((bf16[1024,2048]{1,0:T(8,128)(2,1)}), bf16[64,2048]{1,0:T(8,128)(2,1)}) %reduce-scatter.25.cloned.1.call-update) | async-done | bytes 262160
  603.2 73.4 %reduce-scatter.23.cloned.1.call-done = bf16[64,2048]{1,0:T(8,128)(2,1)} async-done(((bf16[1024,2048]{1,0:T(8,128)(2,1)}), bf16[64,2048]{1,0:T(8,128)(2,1)}) %reduce-scatter.23.cloned.1.call-update) | async-done | bytes 262160 | tf_op jit(solution)/shard_map/reduce_scatter | solution.py:277
  678.4 67.3 %reduce-scatter.19.cloned.1.call-done = bf16[64,1536]{1,0:T(8,128)(2,1)} async-done(((bf16[1024,1536]{1,0:T(8,128)(2,1)}), bf16[64,1536]{1,0:T(8,128)(2,1)}) %reduce-scatter.19.cloned.1.call-update) | async-done | bytes 196624 | tf_op jit(solution)/shard_map/reduce_scatter | solution.py:259
  (157 shorter events, 94.5 us)
Async XLA Ops:
  7.2 77.2 %copy-start.10 = (s32[1,512]{1,0:T(1,128)S(1)}, s32[1,512]{1,0:T(1,128)}, u32[]{:S(2)}) copy-start(s32[1,512]{1,0:T(1,128)} %param.16) | copy-start | bytes 6148
  7.2 93.9 %all-gather.10.cloned.1.call-start = ((), (), s32[]{:S(2)}) async-start(), calls=%async_computation.8 | async-start | bytes 1572864 | tf_op jit(solution)/shard_map/all_gather | solution.py:155
  82.4 66.4 %all-gather.12.cloned.1.call-start = ((), (), s32[]{:S(2)}) async-start(), calls=%async_computation.9 | async-start | bytes 3342336 | tf_op jit(solution)/shard_map/all_gather | solution.py:121
  83.2 104.2 %all-gather.14.cloned.1.call-start = ((), (), s32[]{:S(2)}) async-start(), calls=%async_computation.10 | async-start | bytes 1114112 | tf_op jit(solution)/shard_map/all_gather | solution.py:123
  83.9 125.9 %reduce-scatter.11.cloned.1.call-start = ((), (), s32[]{:S(2)}) async-start(), calls=%async_computation.11 | async-start | bytes 1572864 | tf_op jit(solution)/shard_map/reduce_scatter | solution.py:166
  162.8 28.1 %copy-start.9 = (bf16[8,64,512]{2,1,0:T(8,128)(2,1)}, bf16[8,64,512]{2,1,0:T(8,128)(2,1)S(1)}, u32[]{:S(2)}) copy-start(bf16[8,64,512]{2,1,0:T(8,128)(2,1)S(1)} %convolution_convert_fusion.7) | copy-start | bytes 1572868
  162.9 46.9 %copy-start.1 = (f32[256,1024]{1,0:T(8,128)S(1)}, f32[256,1024]{1,0:T(8,128)}, u32[]{:S(2)}) copy-start(f32[256,1024]{1,0:T(8,128)} %param.15) | copy-start | bytes 3145732
  190.3 22.2 %copy-start.7 = (f32[256,1024]{1,0:T(8,128)S(1)}, f32[256,1024]{1,0:T(8,128)}, u32[]{:S(2)}) copy-start(f32[256,1024]{1,0:T(8,128)} %param.29) | copy-start | bytes 3145732
  190.3 23.9 %copy-start.11 = (bf16[128]{0:T(256)(128)(2,1)S(1)}, bf16[128]{0:T(256)(128)(2,1)}, u32[]{:S(2)}) copy-start(bf16[128]{0:T(256)(128)(2,1)} %param.26) | copy-start | bytes 772
  190.3 72.0 %all-gather.18.cloned.1.call-start = ((), (), s32[]{:S(2)}) async-start(), calls=%async_computation.13 | async-start | bytes 4456448 | tf_op jit(solution)/shard_map/all_gather | solution.py:127
  190.9 93.2 %all-gather.16.cloned.1.call-start = ((), (), s32[]{:S(2)}) async-start(), calls=%async_computation.12 | async-start | bytes 1572864 | tf_op jit(solution)/shard_map/all_gather | solution.py:174
  212.4 95.1 %all-gather.22.cloned.1.call-start = ((), (), s32[]{:S(2)}) async-start(), calls=%async_computation.16 | async-start | bytes 1572864 | tf_op jit(solution)/shard_map/all_gather | solution.py:199
  213.4 146.7 %all-gather.20.cloned.1.call-start = ((), (), s32[]{:S(2)}) async-start(), calls=%async_computation.14 | async-start | bytes 4456448 | tf_op jit(solution)/shard_map/all_gather | solution.py:129
  214.1 178.2 %reduce-scatter.15.cloned.1.call-start = ((), (), s32[]{:S(2)}) async-start(), calls=%async_computation.17 | async-start | bytes 1572864 | tf_op jit(solution)/shard_map/reduce_scatter | solution.py:205
  360.1 9.8 %copy-start.12 = (bf16[1024,2048]{1,0:T(8,128)(2,1)S(1)}, bf16[1024,2048]{1,0:T(8,128)(2,1)}, u32[]{:S(2)}) copy-start(bf16[1024,2048]{1,0:T(8,128)(2,1)} %all-gather.18.cloned.1.call-done) | copy-start | bytes 12582916
  373.3 44.8 %all-gather.24.cloned.1.call-start = ((), (), s32[]{:S(2)}) async-start(), calls=%async_computation.18 | async-start | bytes 1572864 | tf_op jit(solution)/shard_map/all_gather | solution.py:216
  396.6 82.8 %reduce-scatter.21.cloned.1.call-start = ((), (), s32[]{:S(2)}) async-start(), calls=%async_computation.21 | async-start | bytes 1114112 | tf_op jit(solution)/shard_map/reduce_scatter | solution.py:265
  421.1 80.3 %reduce-scatter.17.cloned.1.call-start = ((), (), s32[]{:S(2)}) async-start(), calls=%async_computation.19 | async-start | bytes 1572864 | tf_op jit(solution)/shard_map/reduce_scatter | solution.py:232
  421.3 9.7 %slice-start = ((s8[8388608]{0:T(1024)(128)(4,1)}), s8[4194304]{0:T(1024)(128)(4,1)S(1)}, s32[]{:S(2)}) async-start(s8[8388608]{0:T(1024)(128)(4,1)} %bitcast.78), calls=%async_computation.24 | async-start | bytes 8388608
  424.0 7.1 slice-start.1
  438.9 135.9 %reduce-scatter.13.cloned.1.call-start = ((), (), s32[]{:S(2)}) async-start(), calls=%async_computation.15 | async-start | bytes 1572864 | tf_op jit(solution)/shard_map/reduce_scatter | solution.py:182
  446.2 154.8 %reduce-scatter.25.cloned.1.call-start = ((), (), s32[]{:S(2)}) async-start(), calls=%async_computation.23 | async-start | bytes 4456448
  460.8 215.8 %reduce-scatter.23.cloned.1.call-start = ((), (), s32[]{:S(2)}) async-start(), calls=%async_computation.22 | async-start | bytes 4456448 | tf_op jit(solution)/shard_map/reduce_scatter | solution.py:277
  467.2 278.5 %reduce-scatter.19.cloned.1.call-start = ((), (), s32[]{:S(2)}) async-start(), calls=%async_computation.20 | async-start | bytes 3342336 | tf_op jit(solution)/shard_map/reduce_scatter | solution.py:259
  (10 other events, 28.3 us)
Sparse Core Ops, SparseCore 0:
  82.5 18.5 all-gather.9
  103.4 45.4 all-gather.11
  151.0 36.2 all-gather.13
  190.4 19.3 reduce-scatter.10
  211.8 50.4 all-gather.17
  264.3 19.7 all-gather.15
  286.2 21.2 all-gather.21
  309.7 50.3 all-gather.19
  373.4 18.9 reduce-scatter.14
  396.7 21.2 all-gather.23
  421.6 57.6 reduce-scatter.20
  482.0 19.3 reduce-scatter.16
  504.2 20.3 reduce-scatter.12
  528.4 72.6 reduce-scatter.24
  604.7 71.8 reduce-scatter.22
  680.3 65.3 reduce-scatter.18
where the time goes:
time: 763 us; the launch traced here: 754 us
  waiting for transfers between devices  454 us (60%)
  blocking collectives  152 us (20%)
  matrix products  74.2 us (10%)
  other arithmetic  32.8 us (4%)
  local copies, waits for them, and re-layouts  23.9 us (3%)
  between operations  16.6 us (2%)
    unnamed x2, blocking collectives  123 us
    reduce_scatter x1, waiting for transfers between devices, on_device(): lax.psum_scatter(inner_grad.astype(jnp.bfloat16), 'dp', scatter_dimension...  73.4 us
    reduce_scatter x1, waiting for transfers between devices, on_device(): lax.psum_scatter(qkv_weight_grad.astype(jnp.bfloat16), 'dp', scatter_dime...  67.3 us
    all_gather x1, waiting for transfers between devices, on_device(): lax.all_gather(outer_weight, 'dp', axis=0, tiled=True)  52.6 us
    all_gather x1, waiting for transfers between devices, on_device(): lax.all_gather(qkv_weight, 'dp', axis=0, tiled=True)  47.8 us
    all_gather x1, waiting for transfers between devices, on_device(): lax.all_gather(inner_weight, 'dp', axis=0, tiled=True)  26.1 us
    unnamed x17, waiting for transfers between devices  24.5 us
    all_gather x1, waiting for transfers between devices, on_device(): lax.all_gather(dense_weight, 'dp', axis=0, tiled=True)  24.4 us
  transfers between devices with their start and end apart: 16, of which 15 were waited for; matrix products, arithmetic and copies ran while one was open for 12% of the time, Pallas kernels for 0%

commit v1 on v0

--- a/solution.py
+++ b/solution.py
@@ -8,6 +8,11 @@
 EPSILON = 1e-05
 GELU_C = 0.7978845608028654
 GELU_K = 0.044715
+
+
+def exchange_gather(array, mesh_axis, d):
+    sent = jnp.stack([array] * lax.axis_size(mesh_axis))
+    return jnp.concatenate(lax.all_to_all(sent, mesh_axis, 0, 0), axis=d)
 
 
 def layer_norm(row_data, gain, shift):
@@ -118,7 +123,7 @@
     gathered = (
         lax.all_gather(norm1_gain, "dp", axis=0, tiled=True),
         lax.all_gather(norm1_shift, "dp", axis=0, tiled=True),
-        lax.all_gather(qkv_weight, "dp", axis=0, tiled=True),
+        exchange_gather(qkv_weight, "dp", 0),
         lax.all_gather(qkv_bias, "dp", axis=0, tiled=True),
         lax.all_gather(dense_weight, "dp", axis=0, tiled=True),
         lax.all_gather(dense_bias, "dp", axis=0, tiled=True),

time: 763 us -> 811 us (1.063)
  blocking collectives: 152 us -> 195 us
  matrix products: 74.2 us -> 87.8 us
  waiting for transfers between devices: 454 us -> 441 us
    unnamed x2, blocking collectives: 123 us -> 166 us
    all_gather x1, waiting for transfers between devices: 47.8 us -> 20.8 us  [on_device(): lax.all_gather(qkv_weight, 'dp', axis=0, tiled=True)]
    reduce_scatter x1, waiting for transfers between devices: 2.91 us -> 16.7 us  [on_device(): lax.psum_scatter(dense_grad.astype(jnp.bfloat16), 'dp', scatter_dimension...]
    unnamed x54 -> x62, local copies, waits for them, and re-layouts: 21.7 us -> 16.2 us
  transfers between devices with their start and end apart: 16 -> 17, of which waited for: 15 -> 15; matrix products, arithmetic and copies ran while one was open for 12% -> 14% of each run, Pallas kernels for 0% -> 0%
where the time goes in v1:
time: 811 us; the launch traced here: 802 us
  waiting for transfers between devices  441 us (54%)
  blocking collectives  195 us (24%)
  matrix products  87.8 us (11%)
  other arithmetic  29.1 us (4%)
  local copies, waits for them, and re-layouts  23.5 us (3%)
  between operations  16.6 us (2%)
  starting transfers between devices  8.49 us (1%)
    unnamed x2, blocking collectives  166 us
    reduce_scatter x1, waiting for transfers between devices, on_device(): lax.psum_scatter(inner_grad.astype(jnp.bfloat16), 'dp', scatter_dimension...  73.3 us
    reduce_scatter x1, waiting for transfers between devices, on_device(): lax.psum_scatter(qkv_weight_grad.astype(jnp.bfloat16), 'dp', scatter_dime...  67.3 us
    all_gather x1, waiting for transfers between devices, on_device(): lax.all_gather(outer_weight, 'dp', axis=0, tiled=True)  52.6 us
    all_gather x1, waiting for transfers between devices, on_device(): lax.all_gather(inner_weight, 'dp', axis=0, tiled=True)  26.1 us
    unnamed x17, waiting for transfers between devices  24.4 us
    all_gather x1, waiting for transfers between devices, on_device(): lax.all_gather(dense_weight, 'dp', axis=0, tiled=True)  22.9 us
    dot_general x4, matrix products, rows_product(): lax.dot_general(left, right, (((0,), (0,)), ((), ())), preferred_element_...  22.6 us
  transfers between devices with their start and end apart: 17, of which 15 were waited for; matrix products, arithmetic and copies ran while one was open for 14% of the time, Pallas kernels for 0%

profile of v1, /device:TPU:0, one launch (start us, length us, event | category | flops | bytes accessed | tf_op | source)
XLA Modules:
  0.0 801.9 jit_solution(17110040245635885036)
XLA Ops:
  10.3 7.5 all-to-all-start
  20.5 106.3 %all-reduce.17 = (bf16[1024]{0:T(1024)(128)(2,1)S(1)}, bf16[1024]{0:T(1024)(128)(2,1)S(1)}, bf16[1024]{0:T(1024)(128)(2,1)S(1)}, bf16[1024]{0:T(1024)(128)(2,1)S...) all-reduce(bf16[1024]{0:T(1024)(128)(2,1)S(1)} %dynamic-update-slic, ...), channel_id=1, replica_groups=mesh['dp'=16,'tensor'=2] {'dp'}, use_global_device_ids=true, to_apply=%add.1 | all-reduce | flops 6144 | bytes 24576
  129.8 19.5 %all-gather.10.cloned.1.call-done = bf16[512,1024]{1,0:T(8,128)(2,1)} async-done(((bf16[256,1024]{1,0:T(8,128)(2,1)}), bf16[512,1024]{1,0:T(8,128)(2,1)}) %all-gather.10.cloned.1.call-update) | async-done | bytes 1048592 | tf_op jit(solution)/shard_map/all_gather | solution.py:160
  166.5 22.9 %all-gather.12.cloned.1.call-done = bf16[1024,512]{1,0:T(8,128)(2,1)} async-done(((bf16[64,512]{1,0:T(8,128)(2,1)}), bf16[1024,512]{1,0:T(8,128)(2,1)}) %all-gather.12.cloned.1.call-update) | async-done | bytes 1048592 | tf_op jit(solution)/shard_map/all_gather | solution.py:128
  193.0 18.8 %reduce-scatter.11.cloned.1.call-done = bf16[256,1024]{1,0:T(8,128)(2,1)} async-done(((bf16[512,1024]{1,0:T(8,128)(2,1)}), bf16[256,1024]{1,0:T(8,128)(2,1)}) %reduce-scatter.11.cloned.1.call-update) | async-done | bytes 524304 | tf_op jit(solution)/shard_map/reduce_scatter | solution.py:171
  216.2 22.0 %all-gather = bf16[16,1,128]{2,1,0:T(2,128)(2,1)S(1)} all-gather(bf16[1,1,128]{2,1,0:T(2,128)(2,1)S(1)} %bitcast.95), channel_id=1, replica_groups=mesh['dp'=16,'tensor'=2] {'dp'}, dimensions={0}, use_global_device_ids=true | all-gather | bytes 4352 | tf_op jit(solution)/shard_map/all_gather | solution.py:133
  238.2 26.1 %all-gather.16.cloned.1.call-done = bf16[1024,2048]{1,0:T(8,128)(2,1)} async-done(((bf16[64,2048]{1,0:T(8,128)(2,1)}), bf16[1024,2048]{1,0:T(8,128)(2,1)}) %all-gather.16.cloned.1.call-update) | async-done | bytes 4194320 | tf_op jit(solution)/shard_map/all_gather | solution.py:132
  264.3 21.8 %all-gather.14.cloned.1.call-done = bf16[512,1024]{1,0:T(8,128)(2,1)} async-done(((bf16[256,1024]{1,0:T(8,128)(2,1)}), bf16[512,1024]{1,0:T(8,128)(2,1)}) %all-gather.14.cloned.1.call-update) | async-done | bytes 1048592 | tf_op jit(solution)/shard_map/all_gather | solution.py:179
  286.1 6.8 fusion.44
  293.0 16.5 %all-gather.20.cloned.1.call-done = bf16[512,1024]{1,0:T(8,128)(2,1)} async-done(((bf16[256,1024]{1,0:T(8,128)(2,1)}), bf16[512,1024]{1,0:T(8,128)(2,1)}) %all-gather.20.cloned.1.call-update) | async-done | bytes 1048592 | tf_op jit(solution)/shard_map/all_gather | solution.py:204
  309.4 52.6 %all-gather.18.cloned.1.call-done = bf16[1024,2048]{1,0:T(8,128)(2,1)} async-done(((bf16[64,2048]{1,0:T(8,128)(2,1)}), bf16[1024,2048]{1,0:T(8,128)(2,1)}) %all-gather.18.cloned.1.call-update) | async-done | bytes 4194320 | tf_op jit(solution)/shard_map/all_gather | solution.py:134
  362.0 8.4 %fusion.43 = (bf16[2048]{0:T(1024)(128)(2,1)S(1)}, bf16[512,2048]{1,0:T(8,128)(2,1)S(1)}) fusion(f32[512,2048]{1,0:T(8,128)} %fusion.44, f32[2048]{0:T(1024)S(1)} %bitcast.92, bf16[512,1024]{1,0:T(8,128)(2,1)} %all-gather.20.cloned.1.call-done, bf16[1024,2048]{1,0:T(8,128)(2,1)} %all-gather.18.cloned.1.call-done), kind=kOutput, calls=%fused_computation.102 | convolution fusion | flops 2169501696 | bytes 11546624 | tf_op jit(solution)/shard_map/dot_general | solution.py:206
  375.2 19.0 %reduce-scatter.15.cloned.1.call-done = bf16[256,1024]{1,0:T(8,128)(2,1)} async-done(((bf16[512,1024]{1,0:T(8,128)(2,1)}), bf16[256,1024]{1,0:T(8,128)(2,1)}) %reduce-scatter.15.cloned.1.call-update) | async-done | bytes 524304 | tf_op jit(solution)/shard_map/reduce_scatter | solution.py:210
  399.1 20.8 %all-gather.22.cloned.1.call-done = bf16[512,1024]{1,0:T(8,128)(2,1)} async-done(((bf16[256,1024]{1,0:T(8,128)(2,1)}), bf16[512,1024]{1,0:T(8,128)(2,1)}) %all-gather.22.cloned.1.call-update) | async-done | bytes 1048592 | tf_op jit(solution)/shard_map/all_gather | solution.py:221
  446.7 20.8 %all-gather.24.cloned.1.call-done = bf16[1024,1536]{1,0:T(8,128)(2,1)} async-done(((bf16[64,1536]{1,0:T(8,128)(2,1)}), bf16[1024,1536]{1,0:T(8,128)(2,1)}) %all-gather.24.cloned.1.call-update) | async-done | bytes 3145744 | tf_op jit(solution)/shard_map/all_gather | solution.py:197
  472.8 7.3 convolution_convert_fusion.6
  480.1 7.8 convert_bitcast_fusion
  510.3 16.7 %reduce-scatter.21.cloned.1.call-done = bf16[64,512]{1,0:T(8,128)(2,1)} async-done(((bf16[1024,512]{1,0:T(8,128)(2,1)}), bf16[64,512]{1,0:T(8,128)(2,1)}) %reduce-scatter.21.cloned.1.call-update) | async-done | bytes 65552 | tf_op jit(solution)/shard_map/reduce_scatter | solution.py:270
  528.6 20.6 %reduce-scatter.17.cloned.1.call-done = bf16[256,1024]{1,0:T(8,128)(2,1)} async-done(((bf16[512,1024]{1,0:T(8,128)(2,1)}), bf16[256,1024]{1,0:T(8,128)(2,1)}) %reduce-scatter.17.cloned.1.call-update) | async-done | bytes 524304 | tf_op jit(solution)/shard_map/reduce_scatter | solution.py:237
  550.8 7.1 all-reduce.15
  557.9 60.0 %all-reduce.16 = (bf16[1024]{0:T(1024)(128)(2,1)S(1)}, bf16[1024]{0:T(1024)(128)(2,1)S(1)}, bf16[1024]{0:T(1024)(128)(2,1)S(1)}, bf16[1024]{0:T(1024)(128)(2,1)S...) all-reduce(bf16[1024]{0:T(1024)(128)(2,1)S(1)} %dynamic-update-slic, ...), channel_id=1, replica_groups=mesh['dp'=16,'tensor'=2] {'dp'}, use_global_device_ids=true, to_apply=%add.6 | all-reduce | flops 10240 | bytes 40960
  627.2 21.7 %reduce-scatter.25.cloned.1.call-done = bf16[64,2048]{1,0:T(8,128)(2,1)} async-done(((bf16[1024,2048]{1,0:T(8,128)(2,1)}), bf16[64,2048]{1,0:T(8,128)(2,1)}) %reduce-scatter.25.cloned.1.call-update) | async-done | bytes 262160
  651.1 73.3 %reduce-scatter.23.cloned.1.call-done = bf16[64,2048]{1,0:T(8,128)(2,1)} async-done(((bf16[1024,2048]{1,0:T(8,128)(2,1)}), bf16[64,2048]{1,0:T(8,128)(2,1)}) %reduce-scatter.23.cloned.1.call-update) | async-done | bytes 262160 | tf_op jit(solution)/shard_map/reduce_scatter | solution.py:282
  726.2 67.3 %reduce-scatter.19.cloned.1.call-done = bf16[64,1536]{1,0:T(8,128)(2,1)} async-done(((bf16[1024,1536]{1,0:T(8,128)(2,1)}), bf16[64,1536]{1,0:T(8,128)(2,1)}) %reduce-scatter.19.cloned.1.call-update) | async-done | bytes 196624 | tf_op jit(solution)/shard_map/reduce_scatter | solution.py:264
  (167 shorter events, 113.6 us)
Async XLA Ops:
  7.2 12.8 %copy-start.18 = (bf16[64]{0:T(256)(128)(2,1)S(1)}, bf16[64]{0:T(256)(128)(2,1)}, u32[]{:S(2)}) copy-start(bf16[64]{0:T(256)(128)(2,1)} %param.24) | copy-start | bytes 388
  7.2 13.0 %copy-start.19 = (bf16[64]{0:T(256)(128)(2,1)S(1)}, bf16[64]{0:T(256)(128)(2,1)}, u32[]{:S(2)}) copy-start(bf16[64]{0:T(256)(128)(2,1)} %param.23) | copy-start | bytes 388
  7.3 119.5 %copy-start.1 = (f32[256,1024]{1,0:T(8,128)S(1)}, f32[256,1024]{1,0:T(8,128)}, u32[]{:S(2)}) copy-start(f32[256,1024]{1,0:T(8,128)} %param.15) | copy-start | bytes 3145732
  10.3 139.0 %all-to-all-start = ((bf16[16,64,1536]{2,1,0:T(8,128)(2,1)}), bf16[16,64,1536]{2,1,0:T(8,128)(2,1)}, u32[]{:S(2)}, u32[]{:S(2)}) async-start(bf16[16,64,1536]{2,1,0:T(8,128)(2,1)} %stack.15), calls=%async_computation | async-start | bytes 6291456 | tf_op jit(solution)/shard_map/all_to_all | solution.py:15
  17.8 111.8 %copy-start.10 = (s32[1,512]{1,0:T(1,128)S(1)}, s32[1,512]{1,0:T(1,128)}, u32[]{:S(2)}) copy-start(s32[1,512]{1,0:T(1,128)} %param.16) | copy-start | bytes 6148
  17.8 131.5 %all-gather.10.cloned.1.call-start = ((), (), s32[]{:S(2)}) async-start(), calls=%async_computation.9 | async-start | bytes 1572864 | tf_op jit(solution)/shard_map/all_gather | solution.py:160
  128.3 61.1 %all-gather.12.cloned.1.call-start = ((), (), s32[]{:S(2)}) async-start(), calls=%async_computation.10 | async-start | bytes 1114112 | tf_op jit(solution)/shard_map/all_gather | solution.py:128
  129.0 82.8 %reduce-scatter.11.cloned.1.call-start = ((), (), s32[]{:S(2)}) async-start(), calls=%async_computation.11 | async-start | bytes 1572864 | tf_op jit(solution)/shard_map/reduce_scatter | solution.py:171
  166.4 26.6 %copy-start.9 = (bf16[8,64,512]{2,1,0:T(8,128)(2,1)}, bf16[8,64,512]{2,1,0:T(8,128)(2,1)S(1)}, u32[]{:S(2)}) copy-start(bf16[8,64,512]{2,1,0:T(8,128)(2,1)S(1)} %convolution_convert_fusion.7) | copy-start | bytes 1572868
  192.3 22.2 %copy-start.6 = (f32[256,1024]{1,0:T(8,128)S(1)}, f32[256,1024]{1,0:T(8,128)}, u32[]{:S(2)}) copy-start(f32[256,1024]{1,0:T(8,128)} %param.29) | copy-start | bytes 3145732
  192.3 23.9 %copy-start.12 = (bf16[128]{0:T(256)(128)(2,1)S(1)}, bf16[128]{0:T(256)(128)(2,1)}, u32[]{:S(2)}) copy-start(bf16[128]{0:T(256)(128)(2,1)} %param.26) | copy-start | bytes 772
  192.3 72.0 %all-gather.16.cloned.1.call-start = ((), (), s32[]{:S(2)}) async-start(), calls=%async_computation.13 | async-start | bytes 4456448 | tf_op jit(solution)/shard_map/all_gather | solution.py:132
  192.9 93.2 %all-gather.14.cloned.1.call-start = ((), (), s32[]{:S(2)}) async-start(), calls=%async_computation.12 | async-start | bytes 1572864 | tf_op jit(solution)/shard_map/all_gather | solution.py:179
  214.4 95.0 %all-gather.20.cloned.1.call-start = ((), (), s32[]{:S(2)}) async-start(), calls=%async_computation.16 | async-start | bytes 1572864 | tf_op jit(solution)/shard_map/all_gather | solution.py:204
  215.4 146.6 %all-gather.18.cloned.1.call-start = ((), (), s32[]{:S(2)}) async-start(), calls=%async_computation.14 | async-start | bytes 4456448 | tf_op jit(solution)/shard_map/all_gather | solution.py:134
  216.2 178.1 %reduce-scatter.15.cloned.1.call-start = ((), (), s32[]{:S(2)}) async-start(), calls=%async_computation.17 | async-start | bytes 1572864 | tf_op jit(solution)/shard_map/reduce_scatter | solution.py:210
  375.2 44.8 %all-gather.22.cloned.1.call-start = ((), (), s32[]{:S(2)}) async-start(), calls=%async_computation.18 | async-start | bytes 1572864 | tf_op jit(solution)/shard_map/all_gather | solution.py:221
  398.5 69.0 %all-gather.24.cloned.1.call-start = ((), (), s32[]{:S(2)}) async-start(), calls=%async_computation.19 | async-start | bytes 3342336 | tf_op jit(solution)/shard_map/all_gather | solution.py:197
  399.1 128.0 %reduce-scatter.21.cloned.1.call-start = ((), (), s32[]{:S(2)}) async-start(), calls=%async_computation.22 | async-start | bytes 1114112 | tf_op jit(solution)/shard_map/reduce_scatter | solution.py:270
  432.4 116.8 %reduce-scatter.17.cloned.1.call-start = ((), (), s32[]{:S(2)}) async-start(), calls=%async_computation.20 | async-start | bytes 1572864 | tf_op jit(solution)/shard_map/reduce_scatter | solution.py:237
  472.7 149.8 %reduce-scatter.13.cloned.1.call-start = ((), (), s32[]{:S(2)}) async-start(), calls=%async_computation.15 | async-start | bytes 1572864 | tf_op jit(solution)/shard_map/reduce_scatter | solution.py:187
  480.1 168.8 %reduce-scatter.25.cloned.1.call-start = ((), (), s32[]{:S(2)}) async-start(), calls=%async_computation.24 | async-start | bytes 4456448
  494.5 229.9 %reduce-scatter.23.cloned.1.call-start = ((), (), s32[]{:S(2)}) async-start(), calls=%async_computation.23 | async-start | bytes 4456448 | tf_op jit(solution)/shard_map/reduce_scatter | solution.py:282
  501.1 292.4 %reduce-scatter.19.cloned.1.call-start = ((), (), s32[]{:S(2)}) async-start(), calls=%async_computation.21 | async-start | bytes 3342336 | tf_op jit(solution)/shard_map/reduce_scatter | solution.py:264
  (15 other events, 101.4 us)
Sparse Core Ops, SparseCore 0:
  128.4 20.8 all-gather.9
  151.4 37.8 all-gather.11
  192.4 19.3 reduce-scatter.10
  213.8 50.4 all-gather.15
  266.3 19.7 all-gather.13
  288.1 21.2 all-gather.19
  311.6 50.3 all-gather.17
  375.3 18.9 reduce-scatter.14
  398.6 21.2 all-gather.21
  422.0 45.4 all-gather.23
  471.1 55.8 reduce-scatter.20
  529.8 19.4 reduce-scatter.16
  552.0 20.3 reduce-scatter.12
  576.2 72.6 reduce-scatter.24
  652.6 71.8 reduce-scatter.22
  728.1 65.3 reduce-scatter.18
